TPU v7x, 32 devices: a whole 2x2x4 slice. The times are simulated.
32 devices in a mesh: shard: 2 (over x), ctx: 4 (over z), tp: 4 (over y, core).
Axes of the slice: x: 2, y: 2, z: 4, core: 2. Of those that a mesh axis runs over, the one named last changes fastest.
Arguments:
- tokens: bfloat16 [6, 1024, 1152], P('shard', 'ctx'), may hold values from -6 to 6
- condition: bfloat16 [6, 1152], P('shard'), may hold values from -6 to 6
- ada_weight: bfloat16 [1152, 6912], P('shard'), may hold values from -0.1875 to 0.1875
- ada_bias: float32 [6912], replicated, may hold values from -3 to 3
- qkv_weight: bfloat16 [1152, 16, 216], P('shard', 'tp'), may hold values from -0.1875 to 0.1875
- qv_bias: float32 [16, 144], P('tp'), may hold values from -2 to 2
- out_weight: bfloat16 [1152, 1152], P('tp', 'shard'), may hold values from -1 to 1
- out_bias: float32 [1152], replicated, may hold values from -2 to 2
- up_weight: bfloat16 [1152, 4608], P('shard', 'tp'), may hold values from -0.1875 to 0.1875
- up_bias: float32 [4608], P('tp'), may hold values from -3 to 3
- down_weight: bfloat16 [4608, 1152], P('tp', 'shard'), may hold values from -0.09375 to 0.09375
- down_bias: float32 [1152], replicated, may hold values from -2 to 2
- cotangent: bfloat16 [6, 1024, 1152], P('shard', 'ctx'), may hold values from -6 to 6
Outputs:
- result: bfloat16 [6, 1024, 1152], P('shard', 'ctx')
- grad_tokens: float32 [6, 1024, 1152], P('shard', 'ctx')
- grad_condition: float32 [6, 1152], P('shard')
- grad_ada_weight: float32 [1152, 6912], P('shard')
- grad_ada_bias: float32 [6912], P('shard')
- grad_qkv_weight: float32 [1152, 16, 216], P('shard', 'tp')
- grad_qv_bias: float32 [16, 144], P('tp', 'shard')
- grad_out_weight: float32 [1152, 1152], P('tp', 'shard')
- grad_out_bias: float32 [1152], P('shard')
- grad_up_weight: float32 [1152, 4608], P('shard', 'tp')
- grad_up_bias: float32 [4608], P(('tp', 'shard'))
- grad_down_weight: float32 [4608, 1152], P('tp', 'shard')
- grad_down_bias: float32 [1152], P('shard')
All inputs are finite; a program needn't handle non-finite values.
Results may differ from a plain program's by a relative error of at most 0.02.
The roundings to bfloat16 on the way count: a program that leaves them out, or rounds other values in their place, can miss the bound.
Values may be sent and summed in bfloat16 or wider, within the bound.
A program may use at most 192 MiB of HBM per device.

v0:
```python
import jax
import jax.numpy as jnp
from jax import lax
from jax.sharding import PartitionSpec as P


def layer_norm(values):
    row_mean = jnp.mean(values, -1, keepdims=True)
    centered = values - row_mean
    variance = jnp.mean(centered * centered, -1, keepdims=True)
    return centered * lax.rsqrt(variance + 1e-06)


def modulate(values, shift_row, scale_row):
    return layer_norm(values) * (1.0 + scale_row[:, None, :]) + shift_row[:, None, :]


def gelu_tanh(values):
    return (
        0.5
        * values
        * (1.0 + jnp.tanh(0.7978845608028654 * (values + 0.044715 * values * values * values)))
    )


def silu_act(values):
    return values * jax.nn.sigmoid(values)


def contract_rows(left, right):
    return lax.dot_general(
        left, right, (((0,), (0,)), ((), ())), preferred_element_type=jnp.float32
    )


def contract_cols(left, right):
    return lax.dot_general(
        left, right, (((1,), (1,)), ((), ())), preferred_element_type=jnp.float32
    )


def attend_forward(packed):
    head_size = packed.shape[-1] // 3

    def one_latent(latent_qkv):
        query_part = latent_qkv[..., :head_size]
        key_part = latent_qkv[..., head_size : 2 * head_size]
        value_part = latent_qkv[..., 2 * head_size :]
        scores = jnp.einsum(
            "shd,thd->hst", query_part, key_part, preferred_element_type=jnp.float32
        ) * head_size ** (-0.5)
        row_max = jnp.max(scores, -1, keepdims=True)
        exponent = jnp.exp(scores - row_max)
        exp_total = jnp.sum(exponent, -1, keepdims=True)
        probability = (exponent / exp_total).astype(jnp.bfloat16)
        attended = jnp.einsum(
            "hst,thd->shd", probability, value_part, preferred_element_type=jnp.float32
        )
        log_total = (row_max + jnp.log(exp_total))[..., 0]
        return (attended.astype(jnp.bfloat16), log_total)

    attended, log_total = lax.map(one_latent, packed)
    return (attended, log_total, packed)


def attend_backward(inputs):
    latent_qkv, log_total, grad_out = inputs
    head_size = latent_qkv.shape[-1] // 3
    scale_factor = head_size ** (-0.5)
    query_part = latent_qkv[..., :head_size]
    key_part = latent_qkv[..., head_size : 2 * head_size]
    value_part = latent_qkv[..., 2 * head_size :]
    scores = (
        jnp.einsum("shd,thd->hst", query_part, key_part, preferred_element_type=jnp.float32)
        * scale_factor
    )
    probability = jnp.exp(scores - log_total[..., None])
    prob_low = probability.astype(jnp.bfloat16)
    grad_prob = jnp.einsum("shd,thd->hst", grad_out, value_part, preferred_element_type=jnp.float32)
    row_dot = jnp.sum(probability * grad_prob, -1, keepdims=True)
    grad_scores = (probability * (grad_prob - row_dot)).astype(jnp.bfloat16)
    grad_query = (
        jnp.einsum("hst,thd->shd", grad_scores, key_part, preferred_element_type=jnp.float32)
        * scale_factor
    )
    grad_key = (
        jnp.einsum("hst,shd->thd", grad_scores, query_part, preferred_element_type=jnp.float32)
        * scale_factor
    )
    grad_value = jnp.einsum("hst,shd->thd", prob_low, grad_out, preferred_element_type=jnp.float32)
    return jnp.concatenate([grad_query, grad_key, grad_value], -1).astype(jnp.bfloat16)


def local(
    tokens,
    condition,
    ada_weight,
    ada_bias,
    qkv_weight,
    qv_bias,
    out_weight,
    out_bias,
    up_weight,
    up_bias,
    down_weight,
    down_bias,
    cotangent,
):
    lat_count, local_len, model_width = tokens.shape
    head_local = qkv_weight.shape[1]
    head_size = qv_bias.shape[1] // 2
    row_count = lat_count * local_len
    cond_float = condition.astype(jnp.float32)
    cond_act = silu_act(cond_float).astype(jnp.bfloat16)
    gathered_first, qkv_full, out_full, up_full, down_full = (
        lax.all_gather(ada_weight, "shard", axis=0, tiled=True),
        lax.all_gather(qkv_weight, "shard", axis=0, tiled=True),
        lax.all_gather(out_weight, "shard", axis=1, tiled=True),
        lax.all_gather(up_weight, "shard", axis=0, tiled=True),
        lax.all_gather(down_weight, "shard", axis=1, tiled=True),
    )
    mod_raw = jnp.dot(cond_act, gathered_first, preferred_element_type=jnp.float32)
    modulation = (mod_raw + ada_bias).reshape(lat_count, 6, model_width)
    tok_float = tokens.astype(jnp.float32)
    normed = (
        modulate(tok_float, modulation[:, 0], modulation[:, 1])
        .astype(jnp.bfloat16)
        .reshape(row_count, model_width)
    )
    qkv_bias = jnp.concatenate(
        [
            qv_bias[:, :head_size],
            jnp.zeros((head_local, head_size), jnp.float32),
            qv_bias[:, head_size:],
        ],
        1,
    )
    qkv_flat = qkv_full.reshape(model_width, head_local * 3 * head_size)
    packed = jnp.dot(normed, qkv_flat, preferred_element_type=jnp.float32).reshape(
        lat_count, local_len, head_local, 3 * head_size
    )
    packed = (packed + qkv_bias).astype(jnp.bfloat16)
    attended, log_total, head_packed = attend_forward(
        lax.all_to_all(packed, "ctx", split_axis=2, concat_axis=1, tiled=True)
    )
    attn_rows = lax.all_to_all(attended, "ctx", split_axis=1, concat_axis=2, tiled=True).reshape(
        row_count, head_local * head_size
    )
    branch = (
        lax.psum(
            jnp.dot(attn_rows, out_full, preferred_element_type=jnp.float32).astype(jnp.bfloat16),
            "tp",
        ).astype(jnp.float32)
        + out_bias
    )
    branch = branch.reshape(lat_count, local_len, model_width)
    middle = tok_float + modulation[:, 2][:, None, :] * branch
    normed_two = (
        modulate(middle, modulation[:, 3], modulation[:, 4])
        .astype(jnp.bfloat16)
        .reshape(row_count, model_width)
    )
    up_proj = jnp.dot(normed_two, up_full, preferred_element_type=jnp.float32) + up_bias
    activated = gelu_tanh(up_proj).astype(jnp.bfloat16)
    down_proj = (
        lax.psum(
            jnp.dot(activated, down_full, preferred_element_type=jnp.float32).astype(jnp.bfloat16),
            "tp",
        ).astype(jnp.float32)
        + down_bias
    )
    down_proj = down_proj.reshape(lat_count, local_len, model_width)
    result = (middle + modulation[:, 5][:, None, :] * down_proj).astype(jnp.bfloat16)
    grad_out = cotangent.astype(jnp.float32)
    grad_gate2 = jnp.sum(grad_out * down_proj, 1)
    grad_down = grad_out * modulation[:, 5][:, None, :]
    grad_down_bias = jnp.sum(grad_down, (0, 1))
    grad_down_low = grad_down.astype(jnp.bfloat16).reshape(row_count, model_width)
    grad_act = contract_cols(grad_down_low, down_full)
    grad_down_weight = contract_rows(activated, grad_down_low)
    grad_up = jax.vjp(gelu_tanh, up_proj)[1](grad_act)[0]
    grad_up_bias = jnp.sum(grad_up, 0)
    grad_up_low = grad_up.astype(jnp.bfloat16)
    grad_up_weight = contract_rows(normed_two, grad_up_low)
    grad_normed_two = (
        lax.psum(contract_cols(grad_up_low, up_full).astype(jnp.bfloat16), "tp")
        .astype(jnp.float32)
        .reshape(lat_count, local_len, model_width)
    )
    pull_two = jax.vjp(modulate, middle, modulation[:, 3], modulation[:, 4])[1]
    grad_middle_norm, grad_shift2, grad_scale2 = pull_two(grad_normed_two)
    grad_middle = grad_out + grad_middle_norm
    grad_gate1 = jnp.sum(grad_middle * branch, 1)
    grad_branch = grad_middle * modulation[:, 2][:, None, :]
    grad_out_bias = jnp.sum(grad_branch, (0, 1))
    grad_branch_low = grad_branch.astype(jnp.bfloat16).reshape(row_count, model_width)
    grad_out_weight = contract_rows(attn_rows, grad_branch_low)
    grad_attended = (
        contract_cols(grad_branch_low, out_full)
        .astype(jnp.bfloat16)
        .reshape(lat_count, local_len, head_local, head_size)
    )
    grad_heads = lax.all_to_all(grad_attended, "ctx", split_axis=2, concat_axis=1, tiled=True)
    grad_packed_heads = lax.map(attend_backward, (head_packed, log_total, grad_heads))
    grad_packed = lax.all_to_all(grad_packed_heads, "ctx", split_axis=1, concat_axis=2, tiled=True)
    bias_sums = jnp.sum(grad_packed.astype(jnp.float32), (0, 1))
    grad_qv_bias = jnp.concatenate([bias_sums[:, :head_size], bias_sums[:, 2 * head_size :]], 1)
    grad_packed_rows = grad_packed.reshape(row_count, head_local * 3 * head_size)
    grad_qkv_weight = contract_rows(normed, grad_packed_rows).reshape(
        model_width, head_local, 3 * head_size
    )
    grad_normed = (
        lax.psum(contract_cols(grad_packed_rows, qkv_flat).astype(jnp.bfloat16), "tp")
        .astype(jnp.float32)
        .reshape(lat_count, local_len, model_width)
    )
    pull_one = jax.vjp(modulate, tok_float, modulation[:, 0], modulation[:, 1])[1]
    grad_tokens_norm, grad_shift1, grad_scale1 = pull_one(grad_normed)
    grad_tokens = grad_middle + grad_tokens_norm
    grad_mod_part = jnp.stack(
        [grad_shift1, grad_scale1, grad_gate1, grad_shift2, grad_scale2, grad_gate2], 1
    )
    grad_modulation = (
        lax.psum(grad_mod_part.astype(jnp.bfloat16), "ctx")
        .astype(jnp.float32)
        .reshape(lat_count, 6 * model_width)
    )
    grad_ada_bias_all = jnp.sum(grad_modulation, 0)
    grad_mod_low = grad_modulation.astype(jnp.bfloat16)
    grad_ada_weight_all = contract_rows(cond_act, grad_mod_low)
    grad_cond_act = contract_cols(grad_mod_low, gathered_first)
    ada_stored = (
        lax.psum_scatter(
            grad_ada_weight_all.astype(jnp.bfloat16), "shard", scatter_dimension=0, tiled=True
        ).astype(jnp.float32),
        lax.psum_scatter(
            grad_ada_bias_all.astype(jnp.bfloat16), "shard", scatter_dimension=0, tiled=True
        ).astype(jnp.float32),
    )
    grad_ada_weight = ada_stored[0]
    grad_ada_bias = ada_stored[1]
    grad_condition = jax.vjp(silu_act, cond_float)[1](grad_cond_act)[0]
    stored = (
        lax.psum_scatter(
            grad_qkv_weight.astype(jnp.bfloat16), "shard", scatter_dimension=0, tiled=True
        ).astype(jnp.float32),
        lax.psum_scatter(
            grad_qv_bias.astype(jnp.bfloat16), "shard", scatter_dimension=1, tiled=True
        ).astype(jnp.float32),
        lax.psum_scatter(
            grad_out_weight.astype(jnp.bfloat16), "shard", scatter_dimension=1, tiled=True
        ).astype(jnp.float32),
        lax.psum_scatter(
            grad_out_bias.astype(jnp.bfloat16), "shard", scatter_dimension=0, tiled=True
        ).astype(jnp.float32),
        lax.psum_scatter(
            grad_up_weight.astype(jnp.bfloat16), "shard", scatter_dimension=0, tiled=True
        ).astype(jnp.float32),
        lax.psum_scatter(
            grad_up_bias.astype(jnp.bfloat16), "shard", scatter_dimension=0, tiled=True
        ).astype(jnp.float32),
        lax.psum_scatter(
            grad_down_weight.astype(jnp.bfloat16), "shard", scatter_dimension=1, tiled=True
        ).astype(jnp.float32),
        lax.psum_scatter(
            grad_down_bias.astype(jnp.bfloat16), "shard", scatter_dimension=0, tiled=True
        ).astype(jnp.float32),
    )
    summed = (
        lax.psum(stored[0].astype(jnp.bfloat16), "ctx").astype(jnp.float32),
        lax.psum(stored[1].astype(jnp.bfloat16), "ctx").astype(jnp.float32),
        lax.psum(stored[2].astype(jnp.bfloat16), "ctx").astype(jnp.float32),
        lax.psum(stored[3].astype(jnp.bfloat16), "ctx").astype(jnp.float32),
        lax.psum(stored[4].astype(jnp.bfloat16), "ctx").astype(jnp.float32),
        lax.psum(stored[5].astype(jnp.bfloat16), "ctx").astype(jnp.float32),
        lax.psum(stored[6].astype(jnp.bfloat16), "ctx").astype(jnp.float32),
        lax.psum(stored[7].astype(jnp.bfloat16), "ctx").astype(jnp.float32),
    )
    return (
        result,
        grad_tokens,
        grad_condition,
        grad_ada_weight,
        grad_ada_bias,
        summed[0],
        summed[1],
        summed[2],
        summed[3],
        summed[4],
        summed[5],
        summed[6],
        summed[7],
    )


def solution(mesh):
    return jax.shard_map(
        local,
        mesh=mesh,
        in_specs=(
            P("shard", "ctx", None),
            P("shard", None),
            P("shard", None),
            P(),
            P("shard", "tp", None),
            P("tp", None),
            P("tp", "shard"),
            P(),
            P("shard", "tp"),
            P("tp"),
            P("tp", "shard"),
            P(),
            P("shard", "ctx", None),
        ),
        out_specs=(
            P("shard", "ctx", None),
            P("shard", "ctx", None),
            P("shard", None),
            P("shard", None),
            P("shard"),
            P("shard", "tp", None),
            P("tp", "shard"),
            P("tp", "shard"),
            P("shard"),
            P("shard", "tp"),
            P(("tp", "shard")),
            P("tp", "shard"),
            P("shard"),
        ),
        check_vma=False,
    )
```

profile of v0, /device:TPU:0, one launch (start us, length us, event | category | flops | bytes accessed | tf_op | source)
XLA Modules:
  0.0 1190.2 jit_solution(4975216963075003910)
XLA Ops:
  7.2 3.4 copy.125
  13.2 36.3 %all-gather.8.cloned.1.call-done = bf16[1152,4,216]{2,1,0:T(4,128)(2,1)} async-done(((bf16[576,4,216]{2,1,0:T(4,128)(2,1)}), bf16[1152,4,216]{2,1,0:T(4,128)(2,1)}) %all-gather.8.cloned.1.call-update) | async-done | bytes 1990672 | tf_op jit(solution)/shard_map/all_gather | solution.py:117
  49.6 5.0 copy.126
  54.6 185.9 %all-gather.6.cloned.1.call-done = bf16[1152,6912]{1,0:T(8,128)(2,1)} async-done(((bf16[576,6912]{1,0:T(8,128)(2,1)}), bf16[1152,6912]{1,0:T(8,128)(2,1)}) %all-gather.6.cloned.1.call-update) | async-done | bytes 15925264 | tf_op jit(solution)/shard_map/all_gather | solution.py:116
  240.4 7.7 convolution_add_fusion
  252.9 4.6 all-to-all-start
  257.5 31.7 %all-to-all-done = bf16[3,256,4,216]{1,3,0,2:T(8,128)(2,1)S(1)} async-done(((bf16[3,256,4,216]{1,3,0,2:T(8,128)(2,1)}), bf16[3,256,4,216]{1,3,0,2:T(8,128)(2,1)S(1)}, u32[]{:S(2)}, u32[]{:S(2)}) %all-to-all-start) | async-done | bytes 1327136 | tf_op jit(solution)/shard_map/all_to_all | solution.py:144
  289.3 9.3 while.22
  301.6 3.5 all-to-all-start.1
  305.1 10.4 all-gather
  326.6 41.7 %all-reduce.14.cloned.1.call-done = bf16[768,1152]{1,0:T(8,128)(2,1)} async-done(((bf16[768,1152]{1,0:T(8,128)(2,1)}), bf16[768,1152]{1,0:T(8,128)(2,1)}) %all-reduce.14.cloned.1.call-update) | async-done | bytes 1769488 | tf_op jit(solution)/shard_map/psum | solution.py:150
  375.1 34.1 %all-gather.10.cloned.1.call-done = bf16[1152,1152]{1,0:T(8,128)(2,1)} async-done(((bf16[576,1152]{1,0:T(8,128)(2,1)}), bf16[1152,1152]{1,0:T(8,128)(2,1)}) %all-gather.10.cloned.1.call-update) | async-done | bytes 2654224 | tf_op jit(solution)/shard_map/all_gather | solution.py:119
  409.2 6.7 convolution_add_fusion.1
  416.0 34.2 %all-gather.12.cloned.1.call-done = bf16[1152,1152]{0,1:T(8,128)(2,1)} async-done(((bf16[1152,576]{0,1:T(8,128)(2,1)}), bf16[1152,1152]{0,1:T(8,128)(2,1)}) %all-gather.12.cloned.1.call-update) | async-done | bytes 2654224 | tf_op jit(solution)/shard_map/all_gather | solution.py:120
  450.1 8.5 fusion.73
  458.7 4.2 convolution_convert_fusion.5
  462.9 46.2 %all-reduce.16.cloned.1.call-done = bf16[3,256,1152]{2,1,0:T(8,128)(2,1)} async-done(((bf16[3,256,1152]{2,1,0:T(8,128)(2,1)}), bf16[3,256,1152]{2,1,0:T(8,128)(2,1)}) %all-reduce.16.cloned.1.call-update) | async-done | bytes 1769488 | tf_op jit(solution)/shard_map/psum | solution.py:186
  514.0 2.9 multiply_reduce_fusion.4
  525.8 4.6 all-to-all-start.2
  530.4 12.8 %all-to-all-done.2 = bf16[3,256,4,72]{1,3,0,2:T(8,128)(2,1)} async-done(((bf16[3,256,4,72]{1,3,0,2:T(8,128)(2,1)}), bf16[3,256,4,72]{1,3,0,2:T(8,128)(2,1)}, u32[]{:S(2)}, u32[]{:S(2)}) %all-to-all-start.2) | async-done | bytes 442400 | tf_op jit(solution)/shard_map/all_to_all | solution.py:203
  545.0 23.1 %while.23 = (s32[]{:T(128)}, bf16[3,1024,1,216]{1,3,2,0:T(8,128)(2,1)}, bf16[3,1024,1,216]{1,3,2,0:T(8,128)(2,1)}, f32[3,1,1024]{2,1,0:T(1,128)}, bf16[3,1024,1,72]{1,3,2,0:T(8,128)(2,1)}, /*index=5*/s32[]{:T(128)}) while((s32[]{:T(128)}, bf16[3,1024,1,216]{1,3,2,0:T(8,128)(2,1)}, bf16[3,1024,1,216]{1,3,2,0:T(8,128)(2,1)}, ...), condition=%wide.region_15.16_spmd, body=%wide.region_13.15_spmd.sunk | while | flops 769252352 | bytes 36499580 | solution.py:204
  568.1 4.1 copy.138
  572.1 4.5 all-to-all-start.3
  576.7 3.2 convolution_convert_fusion.8
  582.5 7.2 convolution_convert_fusion.6
  589.7 34.7 %all-to-all-done.3 = bf16[3,1024,1,216]{3,0,2,1:T(4,128)(2,1)} async-done(((bf16[3,1024,1,216]{3,0,2,1:T(4,128)(2,1)}), bf16[3,1024,1,216]{3,0,2,1:T(4,128)(2,1)}, u32[]{:S(2)}, u32[]{:S(2)}) %all-to-all-start.3) | async-done | bytes 1327136 | tf_op jit(solution)/shard_map/all_to_all | solution.py:205
  624.4 4.4 copy.147
  628.7 4.1 copy.140
  632.9 4.2 reshape.332
  637.1 5.3 convolution_convert_fusion.4
  645.0 5.6 convolution_convert_fusion.3
  650.6 4.1 copy.154
  654.7 6.7 convolution_convert_fusion.1
  661.8 6.0 convolution_convert_fusion.2
  678.7 37.2 %all-reduce.18.cloned.1.call-done = (bf16[768,1152]{1,0:T(8,128)(2,1)}, bf16[3,256,1152]{2,1,0:T(8,128)(2,1)}) async-done(((bf16[768,1152]{1,0:T(8,128)(2,1)}, bf16[3,256,1152]{2,1,0:T(8,128)(2,1)}), (bf16[768,1152]{1,0:T(8,128)(2,1)}, bf16[3,256,1152]{2,1,0:T(8,128)(2,1)})) %all-reduce.18.cloned.1.call-update) | async-done | bytes 3538960 | tf_op jit(solution)/shard_map/psum | solution.py:166
  717.7 3.5 fusion.48
  725.5 24.9 %reduce-scatter.17.cloned.1.call-done = bf16[576,864]{1,0:T(8,128)(2,1)} async-done(((bf16[1152,864]{1,0:T(8,128)(2,1)}), bf16[576,864]{1,0:T(8,128)(2,1)}) %reduce-scatter.17.cloned.1.call-update) | async-done | bytes 995344
  752.7 38.3 %reduce-scatter.15.cloned.1.call-done = bf16[1152,576]{0,1:T(8,128)(2,1)} async-done(((bf16[1152,1152]{0,1:T(8,128)(2,1)}), bf16[1152,576]{0,1:T(8,128)(2,1)}) %reduce-scatter.15.cloned.1.call-update) | async-done | bytes 1327120 | tf_op jit(solution)/shard_map/reduce_scatter | solution.py:262
  791.1 40.8 %reduce-scatter.13.cloned.1.call-done = bf16[576,1152]{1,0:T(8,128)(2,1)} async-done(((bf16[1152,1152]{1,0:T(8,128)(2,1)}), bf16[576,1152]{1,0:T(8,128)(2,1)}) %reduce-scatter.13.cloned.1.call-update) | async-done | bytes 1327120 | tf_op jit(solution)/shard_map/reduce_scatter | solution.py:256
  833.3 8.2 all-reduce.8
  846.9 3.1 fusion.43
  853.0 23.4 %all-reduce.6 = (bf16[3,6,1152]{2,0,1:T(4,128)(2,1)}, bf16[4,72]{1,0:T(4,128)(2,1)}, bf16[576]{0:T(1024)(128)(2,1)}, bf16[576]{0:T(1024)(128)(2,1)}, bf16[576]{0:T(1024)(128)(2,1)}) all-reduce(bf16[3,6,1152]{2,0,1:T(4,128)(2,1)} %constant_dynamic-update-slice_fusion.1, ...), channel_id=1, replica_groups=mesh['shard'=2,'ctx'=4,'tp'=4] {'ctx'}, use_global_device_ids=true, to_apply=%region_25.26 | all-reduce | flops 22752 | bytes 91008 | tf_op jit(solution)/shard_map/psum | solution.py:224
  876.4 8.8 convolution_convert_fusion
  893.7 9.6 all-reduce
  905.4 10.6 fusion.68
  918.7 72.3 %all-reduce.20.cloned.1.call-done = (bf16[576,4,216]{0,2,1:T(8,128)(2,1)}, bf16[288,576]{1,0:T(8,128)(2,1)}, bf16[576,1152]{1,0:T(8,128)(2,1)}, bf16[1152,576]{0,1:T(8,128)(2,1)}) async-done(((bf16[576,4,216]{0,2,1:T(8,128)(2,1)}, bf16[288,576]{1,0:T(8,128)(2,1)}, bf16[576,1152]{1,0:T(8,128)(2,1)}, bf16[1152,576]{0,1:T(8,128)(2,1)}), (bf16[576,4,216]{0,2,1:T(8,128)(2,1)}, bf16[288,576]{1,0:T(8,128)(2,1)}, ...) | async-done | bytes 3981328 | tf_op jit(solution)/shard_map/psum | solution.py:270
  999.3 173.7 %reduce-scatter.11.cloned.1.call-done = bf16[576,6912]{1,0:T(8,128)(2,1)} async-done(((bf16[1152,6912]{1,0:T(8,128)(2,1)}), bf16[576,6912]{1,0:T(8,128)(2,1)}) %reduce-scatter.11.cloned.1.call-update) | async-done | bytes 7962640 | tf_op jit(solution)/shard_map/reduce_scatter | solution.py:233
  1172.9 10.3 convert_element_type.196
  (265 shorter events, 130.1 us)
Async XLA Ops:
  7.2 42.4 %all-gather.8.cloned.1.call-start = ((), (), s32[]{:S(2)}) async-start(), calls=%async_computation.10 | async-start | bytes 3538944 | tf_op jit(solution)/shard_map/all_gather | solution.py:117
  10.7 229.8 %all-gather.6.cloned.1.call-start = ((), (), s32[]{:S(2)}) async-start(), calls=%async_computation.9 | async-start | bytes 23887872 | tf_op jit(solution)/shard_map/all_gather | solution.py:116
  12.1 228.3 %copy-start.34 = (bf16[3,1152]{1,0:T(4,128)(2,1)S(1)}, bf16[3,1152]{1,0:T(4,128)(2,1)}, u32[]{:S(2)}) copy-start(bf16[3,1152]{1,0:T(4,128)(2,1)} %param.18) | copy-start | bytes 20740
  12.1 228.3 %copy-start.45 = (f32[6912]{0:T(1024)S(1)}, f32[6912]{0:T(1024)}, u32[]{:S(2)}) copy-start(f32[6912]{0:T(1024)} %param.20) | copy-start | bytes 82948
  12.6 235.7 %copy-start.32 = (f32[3,256]{1,0:T(4,128)}, f32[3,256]{1,0:T(4,128)S(1)}, u32[]{:S(2)}) copy-start(f32[3,256]{1,0:T(4,128)S(1)} %broadcast_multiply_fusion.1) | copy-start | bytes 9220
  13.2 227.2 %copy-start.43 = (f32[3,256]{1,0:T(4,128)}, f32[3,256]{1,0:T(4,128)S(1)}, u32[]{:S(2)}) copy-start(f32[3,256]{1,0:T(4,128)S(1)} %fusion.47) | copy-start | bytes 9220
  13.2 235.1 %copy-start.37 = (f32[3,256]{1,0:T(4,128)}, f32[3,256]{1,0:T(4,128)S(1)}, u32[]{:S(2)}) copy-start(f32[3,256]{1,0:T(4,128)S(1)} %fusion.69) | copy-start | bytes 9220
  248.3 3.4 copy-start.24
  252.9 36.3 %all-to-all-start = ((bf16[3,256,4,216]{1,3,0,2:T(8,128)(2,1)}), bf16[3,256,4,216]{1,3,0,2:T(8,128)(2,1)S(1)}, u32[]{:S(2)}, u32[]{:S(2)}) async-start(bf16[3,256,4,216]{1,3,0,2:T(8,128)(2,1)} %copy.127), calls=%async_computation | async-start | bytes 2654208 | tf_op jit(solution)/shard_map/all_to_all | solution.py:144
  298.7 18.0 %copy-start.9 = (bf16[3,1024,1,216]{1,3,2,0:T(8,128)(2,1)}, bf16[3,1024,1,216]{1,3,2,0:T(8,128)(2,1)S(1)}, u32[]{:S(2)}) copy-start(bf16[3,1024,1,216]{1,3,2,0:T(8,128)(2,1)S(1)} %get-tuple-element.322) | copy-start | bytes 3981316
  298.7 6.4 copy-start.27
  301.6 15.7 %all-to-all-start.1 = ((bf16[4,2,27648]{2,1,0:T(2,128)(2,1)}), bf16[4,2,27648]{2,1,0:T(2,128)(2,1)S(1)}, u32[]{:S(2)}, u32[]{:S(2)}) async-start(bf16[4,2,27648]{2,1,0:T(2,128)(2,1)} %reshape.388), calls=%async_computation.1 | async-start | bytes 884736 | tf_op jit(solution)/shard_map/all_to_all | solution.py:146
  305.0 63.2 %all-reduce.14.cloned.1.call-start = ((), (), s32[]{:S(2)}) async-start(), calls=%async_computation.11 | async-start | bytes 3538944 | tf_op jit(solution)/shard_map/psum | solution.py:150
  316.6 5.9 copy-start.20
  320.1 3.6 copy-start.26
  320.1 4.9 copy-start.10
  322.5 45.7 %copy-start.46 = (f32[1152]{0:T(1024)S(1)}, f32[1152]{0:T(1024)}, u32[]{:S(2)}) copy-start(f32[1152]{0:T(1024)} %param.24) | copy-start | bytes 13828
  322.6 86.7 %all-gather.10.cloned.1.call-start = ((), (), s32[]{:S(2)}) async-start(), calls=%async_computation.12 | async-start | bytes 3981312 | tf_op jit(solution)/shard_map/all_gather | solution.py:119
  323.1 127.0 %all-gather.12.cloned.1.call-start = ((), (), s32[]{:S(2)}) async-start(), calls=%async_computation.13 | async-start | bytes 3981312 | tf_op jit(solution)/shard_map/all_gather | solution.py:120
  323.7 185.4 %all-reduce.16.cloned.1.call-start = ((), (), s32[]{:S(2)}) async-start(), calls=%async_computation.14 | async-start | bytes 3538944 | tf_op jit(solution)/shard_map/psum | solution.py:186
  450.1 8.5 copy-start.49
  458.7 4.2 copy-start.51
  525.8 17.4 %all-to-all-start.2 = ((bf16[3,256,4,72]{1,3,0,2:T(8,128)(2,1)}), bf16[3,256,4,72]{1,3,0,2:T(8,128)(2,1)}, u32[]{:S(2)}, u32[]{:S(2)}) async-start(bf16[3,256,4,72]{1,3,0,2:T(8,128)(2,1)} %copy.134), calls=%async_computation.2 | async-start | bytes 884736 | tf_op jit(solution)/shard_map/all_to_all | solution.py:203
  572.1 52.2 %all-to-all-start.3 = ((bf16[3,1024,1,216]{3,0,2,1:T(4,128)(2,1)}), bf16[3,1024,1,216]{3,0,2,1:T(4,128)(2,1)}, u32[]{:S(2)}, u32[]{:S(2)}) async-start(bf16[3,1024,1,216]{3,0,2,1:T(4,128)(2,1)} %copy.138), calls=%async_computation.3 | async-start | bytes 4194304 | tf_op jit(solution)/shard_map/all_to_all | solution.py:205
  576.6 95.3 %reduce-scatter.19.cloned.1.call-start = ((), (), s32[]{:S(2)}) async-start(), calls=%async_computation.19 | async-start | bytes 1327104
  582.3 133.7 %all-reduce.18.cloned.1.call-start = ((), (), s32[]{:S(2)}) async-start(), calls=%async_computation.20 | async-start | bytes 7077888 | tf_op jit(solution)/shard_map/psum | solution.py:166
  642.4 108.0 %reduce-scatter.17.cloned.1.call-start = ((), (), s32[]{:S(2)}) async-start(), calls=%async_computation.18 | async-start | bytes 3096576
  654.7 136.4 %reduce-scatter.15.cloned.1.call-start = ((), (), s32[]{:S(2)}) async-start(), calls=%async_computation.17 | async-start | bytes 3981312 | tf_op jit(solution)/shard_map/reduce_scatter | solution.py:262
  661.5 6.4 copy-start.50
  661.5 170.4 %reduce-scatter.13.cloned.1.call-start = ((), (), s32[]{:S(2)}) async-start(), calls=%async_computation.16 | async-start | bytes 3981312 | tf_op jit(solution)/shard_map/reduce_scatter | solution.py:256
  667.8 49.9 %copy-start.33 = (f32[3,256]{1,0:T(4,128)S(1)}, f32[3,256]{1,0:T(4,128)}, u32[]{:S(2)}) copy-start(f32[3,256]{1,0:T(4,128)} %copy-done.32) | copy-start | bytes 9220
  667.8 323.2 %all-reduce.20.cloned.1.call-start = ((), (), s32[]{:S(2)}) async-start(), calls=%async_computation.21 | async-start | bytes 8257536 | tf_op jit(solution)/shard_map/psum | solution.py:270
  717.7 4.2 copy-start.17
  717.7 4.2 copy-start.47
  725.5 121.4 %copy-start.2 = (bf16[3,256,1152]{2,1,0:T(8,128)(2,1)S(1)}, bf16[3,256,1152]{2,1,0:T(8,128)(2,1)}, u32[]{:S(2)}) copy-start(bf16[3,256,1152]{2,1,0:T(8,128)(2,1)} %param.17) | copy-start | bytes 5308420
  725.5 121.4 %copy-start.8 = (bf16[3,256,1152]{2,1,0:T(8,128)(2,1)S(1)}, bf16[3,256,1152]{2,1,0:T(8,128)(2,1)}, u32[]{:S(2)}) copy-start(bf16[3,256,1152]{2,1,0:T(8,128)(2,1)} %get-tuple-element.156) | copy-start | bytes 5308420
  831.9 44.5 %copy-start.35 = (bf16[3,1152]{1,0:T(4,128)(2,1)S(1)}, bf16[3,1152]{1,0:T(4,128)(2,1)}, u32[]{:S(2)}) copy-start(bf16[3,1152]{1,0:T(4,128)(2,1)} %param.18) | copy-start | bytes 20740
  832.0 341.0 %reduce-scatter.11.cloned.1.call-start = ((), (), s32[]{:S(2)}) async-start(), calls=%async_computation.15 | async-start | bytes 23887872 | tf_op jit(solution)/shard_map/reduce_scatter | solution.py:233
  841.5 9.1 copy-start.39
  841.5 9.7 copy-start.41
  841.5 10.3 copy-start.44
  841.5 10.9 copy-start.40
  905.4 10.7 copy-start.4
  905.4 10.7 copy-start.25
  905.4 10.7 copy-start.38
  905.4 10.7 copy-start.42
  991.0 4.9 copy-start.19
  993.0 4.5 copy-start.18
  (23 other events, 44.3 us)
Sparse Core Ops, SparseCore 0:
  10.8 38.7 all-gather.7
  51.1 189.2 all-gather.5
  322.7 45.5 all-reduce.13
  369.8 39.4 all-gather.9
  410.7 39.3 all-gather.11
  463.0 46.0 all-reduce.15
  582.4 19.0 reduce-scatter.18
  642.6 73.3 all-reduce.17
  718.8 31.5 reduce-scatter.16
  753.1 37.9 reduce-scatter.14
  793.9 37.9 reduce-scatter.12
  835.0 155.9 all-reduce.19
  994.0 178.8 reduce-scatter.10
where the time goes:
time: 1200 us; the launch traced here: 1190 us
  waiting for transfers between devices  847 us (71%)
  matrix products  103 us (9%)
  local copies, waits for them, and re-layouts  80.4 us (7%)
  other arithmetic  72.6 us (6%)
  blocking collectives  51.7 us (4%)
  starting transfers between devices  18.1 us (2%)
  between operations  16.6 us (1%)
    all_gather x1, waiting for transfers between devices, local(): lax.all_gather(ada_weight, 'shard', axis=0, tiled=True)  186 us
    reduce_scatter x1, waiting for transfers between devices, local(): lax.psum_scatter(grad_ada_weight_all.astype(jnp.bfloat16), 'shard', scatt...  174 us
    psum x1, waiting for transfers between devices, local(): lax.psum(stored[0].astype(jnp.bfloat16), 'ctx').astype(jnp.float32)  72.3 us
    psum x1, waiting for transfers between devices, local(): lax.psum(contract_cols(grad_up_low, up_full).astype(jnp.bfloat16), 'tp')  46.2 us
    psum x1, waiting for transfers between devices, local(): lax.psum(jnp.dot(attn_rows, out_full, preferred_element_type=jnp.float32)...  41.7 us
    reduce_scatter x1, waiting for transfers between devices, local(): lax.psum_scatter(grad_up_weight.astype(jnp.bfloat16), 'shard', scatter_di...  40.8 us
    reduce_scatter x1, waiting for transfers between devices, local(): lax.psum_scatter(grad_down_weight.astype(jnp.bfloat16), 'shard', scatter_...  38.3 us
    psum x1, waiting for transfers between devices, local(): lax.psum(jnp.dot(activated, down_full, preferred_element_type=jnp.float32...  37.2 us
  transfers between devices with their start and end apart: 17, of which 16 were waited for; matrix products, arithmetic and copies ran while one was open for 13% of the time, Pallas kernels for 0%

commit v1 on v0

--- a/solution.py
+++ b/solution.py
@@ -89,6 +89,47 @@
     )
     grad_value = jnp.einsum("hst,shd->thd", prob_low, grad_out, preferred_element_type=jnp.float32)
     return jnp.concatenate([grad_query, grad_key, grad_value], -1).astype(jnp.bfloat16)
+
+
+def swap(values, axis, distance):
+    count = lax.axis_size(axis)
+    return lax.ppermute(values, axis, [(i, i ^ distance) for i in range(count)])
+
+
+def gather_shard(values, axis):
+    if lax.axis_size("shard") != 2:
+        return lax.all_gather(values, "shard", axis=axis, tiled=True)
+    other = swap(values, "shard", 1)
+    first = lax.axis_index("shard") == 0
+    return jnp.concatenate(
+        [jnp.where(first, values, other), jnp.where(first, other, values)], axis
+    )
+
+
+def scatter_shard(values, axis):
+    count = lax.axis_size("shard")
+    if count != 2:
+        return lax.psum_scatter(
+            values.astype(jnp.bfloat16), "shard", scatter_dimension=axis, tiled=True
+        ).astype(jnp.float32)
+    half = values.shape[axis] // 2
+    low = lax.slice_in_dim(values, 0, half, axis=axis)
+    high = lax.slice_in_dim(values, half, 2 * half, axis=axis)
+    first = lax.axis_index("shard") == 0
+    sent = jnp.where(first, high, low).astype(jnp.bfloat16)
+    kept = jnp.where(first, low, high)
+    return kept + swap(sent, "shard", 1).astype(jnp.float32)
+
+
+def sum_axis(values, axis):
+    count = lax.axis_size(axis)
+    if count & (count - 1):
+        return lax.psum(values, axis)
+    distance = 1
+    while distance < count:
+        values = values + swap(values, axis, distance)
+        distance *= 2
+    return values
 
 
 def local(
@@ -110,16 +151,26 @@
     head_local = qkv_weight.shape[1]
     head_size = qv_bias.shape[1] // 2
     row_count = lat_count * local_len
+    shard_count = lax.axis_size("shard")
+    shard_at = lax.axis_index("shard")
+    stored = ada_weight.shape[0]
     cond_float = condition.astype(jnp.float32)
     cond_act = silu_act(cond_float).astype(jnp.bfloat16)
-    gathered_first, qkv_full, out_full, up_full, down_full = (
-        lax.all_gather(ada_weight, "shard", axis=0, tiled=True),
-        lax.all_gather(qkv_weight, "shard", axis=0, tiled=True),
-        lax.all_gather(out_weight, "shard", axis=1, tiled=True),
-        lax.all_gather(up_weight, "shard", axis=0, tiled=True),
-        lax.all_gather(down_weight, "shard", axis=1, tiled=True),
-    )
-    mod_raw = jnp.dot(cond_act, gathered_first, preferred_element_type=jnp.float32)
+    cond_all = lax.all_gather(cond_act, "shard", axis=0, tiled=True) if shard_count != 2 else gather_shard(cond_act, 0)
+    cond_mine = lax.dynamic_slice_in_dim(cond_all, shard_at * stored, stored, 1)
+    mod_part = jnp.dot(cond_mine, ada_weight, preferred_element_type=jnp.float32)
+    if shard_count == 2:
+        first = shard_at == 0
+        mod_low, mod_high = mod_part[:lat_count], mod_part[lat_count:]
+        mod_raw = jnp.where(first, mod_low, mod_high) + swap(
+            jnp.where(first, mod_high, mod_low), "shard", 1
+        )
+    else:
+        mod_raw = lax.psum_scatter(mod_part, "shard", scatter_dimension=0, tiled=True)
+    qkv_full = gather_shard(qkv_weight.reshape(stored, -1), 0)
+    out_full = gather_shard(out_weight, 1)
+    up_full = gather_shard(up_weight, 0)
+    down_full = gather_shard(down_weight, 1)
     modulation = (mod_raw + ada_bias).reshape(lat_count, 6, model_width)
     tok_float = tokens.astype(jnp.float32)
     normed = (
@@ -135,7 +186,7 @@
         ],
         1,
     )
-    qkv_flat = qkv_full.reshape(model_width, head_local * 3 * head_size)
+    qkv_flat = qkv_full
     packed = jnp.dot(normed, qkv_flat, preferred_element_type=jnp.float32).reshape(
         lat_count, local_len, head_local, 3 * head_size
     )
@@ -206,9 +257,7 @@
     bias_sums = jnp.sum(grad_packed.astype(jnp.float32), (0, 1))
     grad_qv_bias = jnp.concatenate([bias_sums[:, :head_size], bias_sums[:, 2 * head_size :]], 1)
     grad_packed_rows = grad_packed.reshape(row_count, head_local * 3 * head_size)
-    grad_qkv_weight = contract_rows(normed, grad_packed_rows).reshape(
-        model_width, head_local, 3 * head_size
-    )
+    grad_qkv_weight = contract_rows(normed, grad_packed_rows)
     grad_normed = (
         lax.psum(contract_cols(grad_packed_rows, qkv_flat).astype(jnp.bfloat16), "tp")
         .astype(jnp.float32)
@@ -220,61 +269,74 @@
     grad_mod_part = jnp.stack(
         [grad_shift1, grad_scale1, grad_gate1, grad_shift2, grad_scale2, grad_gate2], 1
     )
-    grad_modulation = (
-        lax.psum(grad_mod_part.astype(jnp.bfloat16), "ctx")
-        .astype(jnp.float32)
-        .reshape(lat_count, 6 * model_width)
-    )
-    grad_ada_bias_all = jnp.sum(grad_modulation, 0)
-    grad_mod_low = grad_modulation.astype(jnp.bfloat16)
-    grad_ada_weight_all = contract_rows(cond_act, grad_mod_low)
-    grad_cond_act = contract_cols(grad_mod_low, gathered_first)
-    ada_stored = (
-        lax.psum_scatter(
-            grad_ada_weight_all.astype(jnp.bfloat16), "shard", scatter_dimension=0, tiled=True
-        ).astype(jnp.float32),
-        lax.psum_scatter(
-            grad_ada_bias_all.astype(jnp.bfloat16), "shard", scatter_dimension=0, tiled=True
-        ).astype(jnp.float32),
-    )
-    grad_ada_weight = ada_stored[0]
-    grad_ada_bias = ada_stored[1]
+    small = jnp.concatenate(
+        [
+            grad_mod_part.reshape(-1),
+            grad_qv_bias.reshape(-1),
+            grad_out_bias,
+            grad_up_bias,
+            grad_down_bias,
+        ]
+    )
+    small = sum_axis(small, "ctx")
+    mod_count = lat_count * 6 * model_width
+    grad_modulation = small[:mod_count].reshape(lat_count, 6 * model_width)
+    bias_part = small[mod_count:]
+    if shard_count == 2:
+        other = swap(small, "shard", 1)
+        other_mod = other[:mod_count].reshape(lat_count, 6 * model_width)
+        grad_mod_all = jnp.concatenate(
+            [
+                jnp.where(first, grad_modulation, other_mod),
+                jnp.where(first, other_mod, grad_modulation),
+            ],
+            0,
+        )
+        bias_all = bias_part + other[mod_count:]
+    else:
+        grad_mod_all = lax.all_gather(grad_modulation, "shard", axis=0, tiled=True)
+        bias_all = lax.psum(bias_part, "shard")
+    grad_ada_bias_all = jnp.sum(grad_mod_all, 0)
+    grad_ada_bias = lax.dynamic_slice_in_dim(
+        grad_ada_bias_all,
+        shard_at * (6 * model_width // shard_count),
+        6 * model_width // shard_count,
+        0,
+    )
+    grad_mod_low = grad_mod_all.astype(jnp.bfloat16)
+    grad_ada_weight = contract_rows(cond_mine, grad_mod_low)
+    grad_cond_part = contract_cols(grad_mod_low, ada_weight)
+    if shard_count == 2:
+        part_low, part_high = grad_cond_part[:lat_count], grad_cond_part[lat_count:]
+        kept = jnp.where(first, part_low, part_high)
+        got = swap(jnp.where(first, part_high, part_low), "shard", 1)
+        grad_cond_act = jnp.concatenate(
+            [jnp.where(first, kept, got), jnp.where(first, got, kept)], 1
+        )
+    else:
+        grad_cond_act = lax.all_to_all(
+            grad_cond_part, "shard", split_axis=0, concat_axis=1, tiled=True
+        )
     grad_condition = jax.vjp(silu_act, cond_float)[1](grad_cond_act)[0]
-    stored = (
-        lax.psum_scatter(
-            grad_qkv_weight.astype(jnp.bfloat16), "shard", scatter_dimension=0, tiled=True
-        ).astype(jnp.float32),
-        lax.psum_scatter(
-            grad_qv_bias.astype(jnp.bfloat16), "shard", scatter_dimension=1, tiled=True
-        ).astype(jnp.float32),
-        lax.psum_scatter(
-            grad_out_weight.astype(jnp.bfloat16), "shard", scatter_dimension=1, tiled=True
-        ).astype(jnp.float32),
-        lax.psum_scatter(
-            grad_out_bias.astype(jnp.bfloat16), "shard", scatter_dimension=0, tiled=True
-        ).astype(jnp.float32),
-        lax.psum_scatter(
-            grad_up_weight.astype(jnp.bfloat16), "shard", scatter_dimension=0, tiled=True
-        ).astype(jnp.float32),
-        lax.psum_scatter(
-            grad_up_bias.astype(jnp.bfloat16), "shard", scatter_dimension=0, tiled=True
-        ).astype(jnp.float32),
-        lax.psum_scatter(
-            grad_down_weight.astype(jnp.bfloat16), "shard", scatter_dimension=1, tiled=True
-        ).astype(jnp.float32),
-        lax.psum_scatter(
-            grad_down_bias.astype(jnp.bfloat16), "shard", scatter_dimension=0, tiled=True
-        ).astype(jnp.float32),
-    )
+
+    def pick(values, start, size, axis):
+        part = size // shard_count
+        return lax.dynamic_slice_in_dim(
+            values, start + shard_at * part, part, axis
+        )
+
+    bias_width = head_local * 2 * head_size
+    hidden = grad_up_bias.shape[0]
+    qv_sum = bias_all[:bias_width].reshape(head_local, 2 * head_size)
     summed = (
-        lax.psum(stored[0].astype(jnp.bfloat16), "ctx").astype(jnp.float32),
-        lax.psum(stored[1].astype(jnp.bfloat16), "ctx").astype(jnp.float32),
-        lax.psum(stored[2].astype(jnp.bfloat16), "ctx").astype(jnp.float32),
-        lax.psum(stored[3].astype(jnp.bfloat16), "ctx").astype(jnp.float32),
-        lax.psum(stored[4].astype(jnp.bfloat16), "ctx").astype(jnp.float32),
-        lax.psum(stored[5].astype(jnp.bfloat16), "ctx").astype(jnp.float32),
-        lax.psum(stored[6].astype(jnp.bfloat16), "ctx").astype(jnp.float32),
-        lax.psum(stored[7].astype(jnp.bfloat16), "ctx").astype(jnp.float32),
+        lax.psum(scatter_shard(grad_qkv_weight, 0).astype(jnp.bfloat16), "ctx").astype(jnp.float32).reshape(stored, head_local, 3 * head_size),
+        pick(qv_sum, 0, 2 * head_size, 1),
+        lax.psum(scatter_shard(grad_out_weight, 1).astype(jnp.bfloat16), "ctx").astype(jnp.float32),
+        pick(bias_all, bias_width, model_width, 0),
+        lax.psum(scatter_shard(grad_up_weight, 0).astype(jnp.bfloat16), "ctx").astype(jnp.float32),
+        pick(bias_all, bias_width + model_width, hidden, 0),
+        lax.psum(scatter_shard(grad_down_weight, 1).astype(jnp.bfloat16), "ctx").astype(jnp.float32),
+        pick(bias_all, bias_width + model_width + hidden, model_width, 0),
     )
     return (
         result,

time: 1200 us -> 644 us (0.54)
  waiting for transfers between devices: 847 us -> 345 us
  blocking collectives: 51.7 us -> 0 us
  starting transfers between devices: 18.1 us -> 36.9 us
  matrix products: 103 us -> 85 us
  other arithmetic: 72.6 us -> 86.8 us
  local copies, waits for them, and re-layouts: 80.4 us -> 66.3 us
    all_gather x4 -> x0, waiting for transfers between devices: 291 us -> none  [the longest x1 186 us: local(): lax.all_gather(ada_weight, 'shard', axis=0, tiled=True)]
    reduce_scatter x3 -> x0, waiting for transfers between devices: 253 us -> none  [the longest x1 174 us: local(): lax.psum_scatter(grad_ada_weight_all.astype(jnp.bfloat16), 'shard', scatt...]
    psum x1, waiting for transfers between devices: 72.3 us -> 117 us  [local(): lax.psum(scatter_shard(grad_qkv_weight, 0).astype(jnp.bfloat16), 'ctx')]
    ppermute x0 -> x14, waiting for transfers between devices: none -> 28.3 us  [swap(): return lax.ppermute(values, axis, [(i, i ^ distance) for i in range(count)])]
    unnamed x15 -> x4, waiting for transfers between devices: 26.8 us -> 0.07 us
    psum x1 -> x0, blocking collectives: 23.4 us -> none  [local(): lax.psum(grad_mod_part.astype(jnp.bfloat16), 'ctx').astype(jnp.float32)]
    psum x1, waiting for transfers between devices: 37.2 us -> 56.7 us  [local(): lax.psum(jnp.dot(activated, down_full, preferred_element_type=jnp.float32...]
    ppermute x0 -> x14, starting transfers between devices: none -> 18.9 us  [swap(): return lax.ppermute(values, axis, [(i, i ^ distance) for i in range(count)])]
  transfers between devices with their start and end apart: 17 -> 22, of which waited for: 16 -> 11; matrix products, arithmetic and copies ran while one was open for 13% -> 29% of each run, Pallas kernels for 0% -> 0%
where the time goes in v1:
time: 644 us; the launch traced here: 635 us
  waiting for transfers between devices  345 us (54%)
  other arithmetic  86.8 us (13%)
  matrix products  85 us (13%)
  local copies, waits for them, and re-layouts  66.3 us (10%)
  starting transfers between devices  36.9 us (6%)
  between operations  15.1 us (2%)
    psum x1, waiting for transfers between devices, local(): lax.psum(scatter_shard(grad_qkv_weight, 0).astype(jnp.bfloat16), 'ctx')  117 us
    psum x1, waiting for transfers between devices, local(): lax.psum(jnp.dot(activated, down_full, preferred_element_type=jnp.float32...  56.7 us
    psum x1, waiting for transfers between devices, local(): lax.psum(jnp.dot(attn_rows, out_full, preferred_element_type=jnp.float32)...  38 us
    psum x1, waiting for transfers between devices, local(): lax.psum(contract_cols(grad_up_low, up_full).astype(jnp.bfloat16), 'tp')  35.9 us
    ppermute x14, waiting for transfers between devices, swap(): return lax.ppermute(values, axis, [(i, i ^ distance) for i in range(count)])  28.3 us
    all_to_all x1, waiting for transfers between devices, local(): lax.all_to_all(grad_packed_heads, 'ctx', split_axis=1, concat_axis=2, til...  28.2 us
    all_to_all x1, waiting for transfers between devices, local(): lax.all_to_all(packed, 'ctx', split_axis=2, concat_axis=1, tiled=True)  25.8 us
    dot_general x5, matrix products, contract_rows(): lax.dot_general(left, right, (((0,), (0,)), ((), ())), preferred_element_...  24.4 us
  transfers between devices with their start and end apart: 22, of which 11 were waited for; matrix products, arithmetic and copies ran while one was open for 29% of the time, Pallas kernels for 0%

profile of v1, /device:TPU:0, one launch (start us, length us, event | category | flops | bytes accessed | tf_op | source)
XLA Modules:
  0.0 635.3 jit_solution(15593193496477154573)
XLA Ops:
  8.1 3.0 collective-permute-start
  16.5 4.4 fusion.83
  23.2 16.3 %collective-permute-done.1 = f32[3,6912]{1,0:T(4,128)S(1)} collective-permute-done((f32[3,6912]{1,0:T(4,128)S(1)}, f32[3,6912]{1,0:T(4,128)S(1)}, u32[]{:S(2)}, u32[]{:S(2)}) %collective-permute-start.1) | collective-permute-done | bytes 82976 | tf_op jit(solution)/shard_map/ppermute | solution.py:96
  40.9 2.5 fusion.40
  48.7 4.0 add_convert_fusion.4
  53.8 4.9 all-to-all-start
  63.5 25.8 %all-to-all-done = bf16[3,256,4,216]{1,3,0,2:T(8,128)(2,1)S(1)} async-done(((bf16[3,256,4,216]{1,3,0,2:T(8,128)(2,1)}), bf16[3,256,4,216]{1,3,0,2:T(8,128)(2,1)S(1)}, u32[]{:S(2)}, u32[]{:S(2)}) %all-to-all-start) | async-done | bytes 1327136 | tf_op jit(solution)/shard_map/all_to_all | solution.py:195
  89.5 9.3 %while.22 = (s32[]{:T(128)}, bf16[3,1024,1,72]{1,3,2,0:T(8,128)(2,1)S(1)}, f32[3,1,1024]{2,1,0:T(1,128)}, bf16[3,1024,1,216]{1,3,2,0:T(8,128)(2,1)S(1)}, s32[]{:T(128)}) while((s32[]{:T(128)}, bf16[3,1024,1,72]{1,3,2,0:T(8,128)(2,1)S(1)}, f32[3,1,1024]{2,1,0:T(1,128)}, bf16[3,1024,1,216]{1,3,2,0:T(8,128)(2,1)S(1)}, s32[]{:T(128)}) %tuple.107), condition=%wide.region_5.6_spmd, body=%wide.region_2.5_spmd.sunk | while | flops 311499776 | bytes 14098513 | solution.py:62
  101.7 3.5 all-to-all-start.1
  107.9 9.5 %all-to-all-done.1 = bf16[4,2,27648]{2,1,0:T(2,128)(2,1)S(1)} async-done(((bf16[4,2,27648]{2,1,0:T(2,128)(2,1)}), bf16[4,2,27648]{2,1,0:T(2,128)(2,1)S(1)}, u32[]{:S(2)}, u32[]{:S(2)}) %all-to-all-start.1) | async-done | bytes 442400 | tf_op jit(solution)/shard_map/all_to_all | solution.py:197
  123.6 3.1 broadcast_select_fusion.3
  126.7 3.2 broadcast_select_fusion.1
  129.9 38.0 %all-reduce.7.cloned.1.call-done = bf16[768,1152]{1,0:T(8,128)(2,1)} async-done(((bf16[768,1152]{1,0:T(8,128)(2,1)}), bf16[768,1152]{1,0:T(8,128)(2,1)}) %all-reduce.7.cloned.1.call-update) | async-done | bytes 1769488 | tf_op jit(solution)/shard_map/psum | solution.py:201
  173.8 2.7 convolution_add_fusion
  176.5 5.0 fusion.86
  181.5 6.9 %fusion.94 = (f32[1152]{0:T(1024)}, bf16[768,1152]{1,0:T(8,128)(2,1)S(1)}) fusion(f32[768,1152]{1,0:T(8,128)S(1)} %convolution_add_fusion, bf16[768,1152]{1,0:T(8,128)(2,1)S(1)} %bitcast.203, bf16[1152,576]{0,1:T(8,128)(2,1)S(1)} %copy-done.29, bf16[1152,576]{0,1:T(8,128)(2,1)S(1)} %copy-done.28), kind=kOutput, calls=%fused_computation.200 | convolution fusion | flops 2065857408 | bytes 9736704 | tf_op jit(solution)/shard_map/dot_general | solution.py:37
  188.4 3.8 convolution_convert_fusion.1
  192.3 4.0 select_convert_fusion
  197.8 4.9 fusion.60
  202.6 35.9 %all-reduce.9.cloned.1.call-done = bf16[3,256,1152]{2,1,0:T(8,128)(2,1)} async-done(((bf16[3,256,1152]{2,1,0:T(8,128)(2,1)}), bf16[3,256,1152]{2,1,0:T(8,128)(2,1)}) %all-reduce.9.cloned.1.call-update) | async-done | bytes 1769488 | tf_op jit(solution)/shard_map/psum | solution.py:237
  243.3 2.9 multiply_reduce_fusion.4
  255.3 4.8 all-to-all-start.2
  260.1 7.2 %convolution_convert_fusion.2 = bf16[768,1152]{1,0:T(8,128)(2,1)} fusion(bf16[1152,576]{0,1:T(8,128)(2,1)} %get-tuple-element.192, bf16[1152,576]{0,1:T(8,128)(2,1)} %get-tuple-element.191, f32[768,1152]{1,0:T(8,128)} %copy-done.70), kind=kOutput, calls=%fused_computation.96 | convolution fusion | flops 2052587520 | bytes 7962624 | tf_op jit(solution)/shard_map/dot_general | solution.py:218
  267.3 5.6 all-to-all-done.2
  274.6 23.0 %while.23 = (s32[]{:T(128)}, bf16[3,1024,1,216]{1,3,2,0:T(8,128)(2,1)}, bf16[3,1024,1,216]{1,3,2,0:T(8,128)(2,1)}, f32[3,1,1024]{2,1,0:T(1,128)}, bf16[3,1024,1,72]{1,3,2,0:T(8,128)(2,1)}, /*index=5*/s32[]{:T(128)}) while((s32[]{:T(128)}, bf16[3,1024,1,216]{1,3,2,0:T(8,128)(2,1)}, bf16[3,1024,1,216]{1,3,2,0:T(8,128)(2,1)}, ...), condition=%wide.region_15.16_spmd, body=%wide.region_13.15_spmd.sunk | while | flops 769252352 | bytes 36499580 | solution.py:255
  297.7 4.1 copy.179
  301.8 4.5 all-to-all-start.3
  310.4 3.9 select_convert_fusion.1
  316.6 3.8 collective-permute-done.11
  321.4 4.4 add_convert_fusion.2
  325.8 28.2 %all-to-all-done.3 = bf16[3,1024,1,216]{3,0,2,1:T(4,128)(2,1)} async-done(((bf16[3,1024,1,216]{3,0,2,1:T(4,128)(2,1)}), bf16[3,1024,1,216]{3,0,2,1:T(4,128)(2,1)}, u32[]{:S(2)}, u32[]{:S(2)}) %all-to-all-start.3) | async-done | bytes 1327136 | tf_op jit(solution)/shard_map/all_to_all | solution.py:256
  354.0 4.5 copy.190
  358.5 4.1 copy.181
  362.6 4.2 reshape.364
  366.8 5.3 convolution_convert_fusion
  372.2 4.5 add_convert_fusion.3
  380.4 4.0 fusion.95
  389.0 56.7 %all-reduce.11.cloned.1.call-done = (bf16[768,1152]{1,0:T(8,128)(2,1)}, bf16[3,256,1152]{2,1,0:T(8,128)(2,1)}) async-done(((bf16[768,1152]{1,0:T(8,128)(2,1)}, bf16[3,256,1152]{2,1,0:T(8,128)(2,1)}), (bf16[768,1152]{1,0:T(8,128)(2,1)}, bf16[3,256,1152]{2,1,0:T(8,128)(2,1)})) %all-reduce.11.cloned.1.call-update) | async-done | bytes 3538960 | tf_op jit(solution)/shard_map/psum | solution.py:217
  445.7 3.0 fusion.46
  448.8 2.7 fusion.51
  453.0 2.8 fusion.33
  459.7 3.7 add_convert_fusion.5
  470.0 8.2 %collective-permute-done.7 = f32[24768]{0:T(1024)S(1)} collective-permute-done((f32[24768]{0:T(1024)S(1)}, f32[24768]{0:T(1024)S(1)}, u32[]{:S(2)}, u32[]{:S(2)}) %collective-permute-start.7) | collective-permute-done | bytes 99104 | tf_op jit(solution)/shard_map/ppermute | solution.py:96
  479.8 4.1 add_add_fusion.2
  486.5 5.5 fusion.64
  493.3 8.2 %fusion.63 = f32[576,6912]{1,0:T(8,128)} fusion(bf16[3,6912]{1,0:T(4,128)(2,1)S(1)} %get-tuple-element.202, bf16[3,6912]{1,0:T(4,128)(2,1)S(1)} %get-tuple-element.200, s32[]{:T(128)S(6)} %select_n.170, bf16[3,1152]{1,0:T(4,128)(2,1)S(1)} %copy-done.51, bf16[3,1152]{1,0:T(4,128)(2,1)S(1)} %copy-done.49), kind=kOutput, calls=%fused_computation.137 | convolution fusion | flops 47955456 | bytes 16022020 | tf_op jit(solution)/shard_map/dot_general | solution.py:31
  502.9 117.2 %all-reduce.13.cloned.1.call-done = (bf16[576,4,216]{0,2,1:T(8,128)(2,1)}, bf16[288,576]{1,0:T(8,128)(2,1)}, bf16[576,1152]{1,0:T(8,128)(2,1)}, bf16[1152,576]{0,1:T(8,128)(2,1)}) async-done(((bf16[576,4,216]{0,2,1:T(8,128)(2,1)}, bf16[288,576]{1,0:T(8,128)(2,1)}, bf16[576,1152]{1,0:T(8,128)(2,1)}, bf16[1152,576]{0,1:T(8,128)(2,1)}), (bf16[576,4,216]{0,2,1:T(8,128)(2,1)}, bf16[288,576]{1,0:T(8,128)(2,1)}, ...) | async-done | bytes 3981328 | tf_op jit(solution)/shard_map/psum | solution.py:332
  622.1 2.8 reshape.375
  (319 shorter events, 128.1 us)
Async XLA Ops:
  7.2 8.7 %copy-start.52 = (bf16[3,1152]{1,0:T(4,128)(2,1)S(1)}, bf16[3,1152]{1,0:T(4,128)(2,1)}, u32[]{:S(2)}) copy-start(bf16[3,1152]{1,0:T(4,128)(2,1)} %param.18) | copy-start | bytes 20740
  7.2 7.5 %copy-start = (bf16[3,256,1152]{2,1,0:T(8,128)(2,1)S(1)}, bf16[3,256,1152]{2,1,0:T(8,128)(2,1)}, u32[]{:S(2)}) copy-start(bf16[3,256,1152]{2,1,0:T(8,128)(2,1)} %param.17) | copy-start | bytes 5308420
  7.2 8.1 %copy-start.68 = (f32[4,144]{1,0:T(4,128)S(1)}, f32[4,144]{1,0:T(4,128)}, u32[]{:S(2)}) copy-start(f32[4,144]{1,0:T(4,128)} %param.22) | copy-start | bytes 6916
  8.1 7.8 %collective-permute-start = (bf16[3,1152]{1,0:T(4,128)(2,1)S(1)}, bf16[3,1152]{1,0:T(4,128)(2,1)S(1)}, u32[]{:S(2)}, u32[]{:S(2)}) collective-permute-start(bf16[3,1152]{1,0:T(4,128)(2,1)S(1)} %fusion.68), channel_id=1, source_target_pairs={{0,16},{16,0},{1,17},{17,1},{2,18},{18,2},{3,19},{19,3},{4,20},{20... | collective-permute-start | bytes 20744 | tf_op jit(solution)/shard_map/ppermute | solution.py:96
  12.8 30.6 %collective-permute-start.2 = (bf16[576,864]{1,0:T(8,128)(2,1)S(1)}, bf16[576,864]{1,0:T(8,128)(2,1)}, u32[]{:S(2)}, u32[]{:S(2)}) collective-permute-start(bf16[576,864]{1,0:T(8,128)(2,1)S(1)} %copy.166), channel_id=1, source_target_pairs={{0,16},{16,0},{1,17},{17,1},{2,18},{18,2},{3,19},{19,3},{4,20},{20... | collective-permute-start | bytes 2985992 | tf_op jit(solution)/shard_map/ppermute | solution.py:96
  14.7 26.2 %copy-start.45 = (f32[3,256]{1,0:T(4,128)}, f32[3,256]{1,0:T(4,128)S(1)}, u32[]{:S(2)}) copy-start(f32[3,256]{1,0:T(4,128)S(1)} %broadcast_multiply_fusion.1) | copy-start | bytes 9220
  15.3 25.6 %copy-start.58 = (f32[3,256]{1,0:T(4,128)}, f32[3,256]{1,0:T(4,128)S(1)}, u32[]{:S(2)}) copy-start(f32[3,256]{1,0:T(4,128)S(1)} %fusion.72) | copy-start | bytes 9220
  16.5 22.9 %copy-start.64 = (f32[6912]{0:T(1024)S(1)}, f32[6912]{0:T(1024)}, u32[]{:S(2)}) copy-start(f32[6912]{0:T(1024)} %param.20) | copy-start | bytes 82948
  21.0 18.4 %collective-permute-start.1 = (f32[3,6912]{1,0:T(4,128)S(1)}, f32[3,6912]{1,0:T(4,128)S(1)}, u32[]{:S(2)}, u32[]{:S(2)}) collective-permute-start(f32[3,6912]{1,0:T(4,128)S(1)} %slice_select_fusion), channel_id=1, source_target_pairs={{0,16},{16,0},{1,17},{17,1},{2,18},{18,2},{3,19},{19,3},{4,20},{20... | collective-permute-start | bytes 248840 | tf_op jit(solution)/shard_map/ppermute | solution.py:96
  52.7 8.6 %copy-start.11 = (bf16[3,256,1152]{2,1,0:T(8,128)(2,1)S(1)}, bf16[3,256,1152]{2,1,0:T(8,128)(2,1)}, u32[]{:S(2)}) copy-start(bf16[3,256,1152]{2,1,0:T(8,128)(2,1)} %param.29) | copy-start | bytes 5308420
  53.8 35.5 %all-to-all-start = ((bf16[3,256,4,216]{1,3,0,2:T(8,128)(2,1)}), bf16[3,256,4,216]{1,3,0,2:T(8,128)(2,1)S(1)}, u32[]{:S(2)}, u32[]{:S(2)}) async-start(bf16[3,256,4,216]{1,3,0,2:T(8,128)(2,1)} %copy.169), calls=%async_computation | async-start | bytes 2654208 | tf_op jit(solution)/shard_map/all_to_all | solution.py:195
  58.7 48.0 %collective-permute-start.3 = (bf16[288,576]{1,0:T(8,128)(2,1)}, bf16[288,576]{1,0:T(8,128)(2,1)}, u32[]{:S(2)}, u32[]{:S(2)}) collective-permute-start(bf16[288,576]{1,0:T(8,128)(2,1)} %param.23), channel_id=1, source_target_pairs={{0,16},{16,0},{1,17},{17,1},{2,18},{18,2},{3,19},{19,3},{4,20},{20... | collective-permute-start | bytes 995336 | tf_op jit(solution)/shard_map/ppermute | solution.py:96
  59.2 64.3 %collective-permute-start.4 = (bf16[576,1152]{1,0:T(8,128)(2,1)}, bf16[576,1152]{1,0:T(8,128)(2,1)}, u32[]{:S(2)}, u32[]{:S(2)}) collective-permute-start(bf16[576,1152]{1,0:T(8,128)(2,1)} %param.25), channel_id=1, source_target_pairs={{0,16},{16,0},{1,17},{17,1},{2,18},{18,2},{3,19},{19,3},{4,20},{20... | collective-permute-start | bytes 3981320 | tf_op jit(solution)/shard_map/ppermute | solution.py:96
  60.7 66.0 %collective-permute-start.5 = (bf16[1152,576]{0,1:T(8,128)(2,1)}, bf16[1152,576]{0,1:T(8,128)(2,1)}, u32[]{:S(2)}, u32[]{:S(2)}) collective-permute-start(bf16[1152,576]{0,1:T(8,128)(2,1)} %param.27), channel_id=1, source_target_pairs={{0,16},{16,0},{1,17},{17,1},{2,18},{18,2},{3,19},{19,3},{4,20},{20... | collective-permute-start | bytes 3981320 | tf_op jit(solution)/shard_map/ppermute | solution.py:96
  98.8 21.0 %copy-start.7 = (bf16[3,1024,1,216]{1,3,2,0:T(8,128)(2,1)}, bf16[3,1024,1,216]{1,3,2,0:T(8,128)(2,1)S(1)}, u32[]{:S(2)}) copy-start(bf16[3,1024,1,216]{1,3,2,0:T(8,128)(2,1)S(1)} %get-tuple-element.340) | copy-start | bytes 3981316
  98.8 6.6 %copy-start.60 = (f32[3,1,1152]{2,1,0:T(1,128)S(1)}, f32[3,1,1152]{2,1,0:T(1,128)}, u32[]{:S(2)}) copy-start(f32[3,1,1152]{2,1,0:T(1,128)} %get-tuple-element.206) | copy-start | bytes 41476
  98.8 6.7 %copy-start.61 = (f32[3,1,1152]{2,1,0:T(1,128)S(1)}, f32[3,1,1152]{2,1,0:T(1,128)}, u32[]{:S(2)}) copy-start(f32[3,1,1152]{2,1,0:T(1,128)} %get-tuple-element.207) | copy-start | bytes 41476
  101.7 15.7 %all-to-all-start.1 = ((bf16[4,2,27648]{2,1,0:T(2,128)(2,1)}), bf16[4,2,27648]{2,1,0:T(2,128)(2,1)S(1)}, u32[]{:S(2)}, u32[]{:S(2)}) async-start(bf16[4,2,27648]{2,1,0:T(2,128)(2,1)} %reshape.412), calls=%async_computation.1 | async-start | bytes 884736 | tf_op jit(solution)/shard_map/all_to_all | solution.py:197
  105.2 62.7 %all-reduce.7.cloned.1.call-start = ((), (), s32[]{:S(2)}) async-start(), calls=%async_computation.4 | async-start | bytes 3538944 | tf_op jit(solution)/shard_map/psum | solution.py:201
  107.9 15.6 %copy-start.38 = (bf16[288,576]{1,0:T(8,128)(2,1)}, bf16[288,576]{1,0:T(8,128)(2,1)S(1)}, u32[]{:S(2)}) copy-start(bf16[288,576]{1,0:T(8,128)(2,1)S(1)} %get-tuple-element.195) | copy-start | bytes 995332
  107.9 15.6 %copy-start.40 = (bf16[288,576]{1,0:T(8,128)(2,1)}, bf16[288,576]{1,0:T(8,128)(2,1)S(1)}, u32[]{:S(2)}) copy-start(bf16[288,576]{1,0:T(8,128)(2,1)S(1)} %get-tuple-element.196) | copy-start | bytes 995332
  123.5 115.0 %all-reduce.9.cloned.1.call-start = ((), (), s32[]{:S(2)}) async-start(), calls=%async_computation.5 | async-start | bytes 3538944 | tf_op jit(solution)/shard_map/psum | solution.py:237
  126.7 41.2 %copy-start.66 = (f32[1152]{0:T(1024)S(1)}, f32[1152]{0:T(1024)}, u32[]{:S(2)}) copy-start(f32[1152]{0:T(1024)} %param.24) | copy-start | bytes 13828
  196.3 125.1 %collective-permute-start.13 = (bf16[1152,576]{0,1:T(8,128)(2,1)}, bf16[1152,576]{0,1:T(8,128)(2,1)}, u32[]{:S(2)}, u32[]{:S(2)}) collective-permute-start(bf16[1152,576]{0,1:T(8,128)(2,1)} %select_convert_fusion), channel_id=1, source_target_pairs={{0,16},{16,0},{1,17},{17,1},{2,18},{18,2},{3,19},{19,3},{4,20},{20... | collective-permute-start | bytes 3981320 | tf_op jit(solution)/shard_map/ppermute | solution.py:96
  255.3 17.5 %all-to-all-start.2 = ((bf16[3,256,4,72]{1,3,0,2:T(8,128)(2,1)}), bf16[3,256,4,72]{1,3,0,2:T(8,128)(2,1)}, u32[]{:S(2)}, u32[]{:S(2)}) async-start(bf16[3,256,4,72]{1,3,0,2:T(8,128)(2,1)} %copy.175), calls=%async_computation.2 | async-start | bytes 884736 | tf_op jit(solution)/shard_map/all_to_all | solution.py:254
  301.8 52.2 %all-to-all-start.3 = ((bf16[3,1024,1,216]{3,0,2,1:T(4,128)(2,1)}), bf16[3,1024,1,216]{3,0,2,1:T(4,128)(2,1)}, u32[]{:S(2)}, u32[]{:S(2)}) async-start(bf16[3,1024,1,216]{3,0,2,1:T(4,128)(2,1)} %copy.179), calls=%async_computation.3 | async-start | bytes 4194304 | tf_op jit(solution)/shard_map/all_to_all | solution.py:256
  306.2 139.4 %all-reduce.11.cloned.1.call-start = ((), (), s32[]{:S(2)}) async-start(), calls=%async_computation.6 | async-start | bytes 7077888 | tf_op jit(solution)/shard_map/psum | solution.py:217
  308.6 6.2 copy-start.55
  308.7 6.8 %copy-start.56 = (f32[3,1152]{1,0:T(4,128)S(1)}, f32[3,1152]{1,0:T(4,128)}, u32[]{:S(2)}) copy-start(f32[3,1152]{1,0:T(4,128)} %get-tuple-element.152) | copy-start | bytes 41476
  308.7 7.4 %copy-start.54 = (f32[3,1152]{1,0:T(4,128)S(1)}, f32[3,1152]{1,0:T(4,128)}, u32[]{:S(2)}) copy-start(f32[3,1152]{1,0:T(4,128)} %get-tuple-element.155) | copy-start | bytes 41476
  308.8 11.6 %collective-permute-start.11 = (bf16[288,576]{1,0:T(8,128)(2,1)S(1)}, bf16[288,576]{1,0:T(8,128)(2,1)S(1)}, u32[]{:S(2)}, u32[]{:S(2)}) collective-permute-start(bf16[288,576]{1,0:T(8,128)(2,1)S(1)} %select_convert_fusion.3), channel_id=1, source_target_pairs={{0,16},{16,0},{1,17},{17,1},{2,18},{18,2},{3,19},{19,3},{4,20},{20... | collective-permute-start | bytes 995336 | tf_op jit(solution)/shard_map/ppermute | solution.py:96
  314.2 58.0 %collective-permute-start.12 = (bf16[576,1152]{1,0:T(8,128)(2,1)}, bf16[576,1152]{1,0:T(8,128)(2,1)}, u32[]{:S(2)}, u32[]{:S(2)}) collective-permute-start(bf16[576,1152]{1,0:T(8,128)(2,1)} %select_convert_fusion.1), channel_id=1, source_target_pairs={{0,16},{16,0},{1,17},{17,1},{2,18},{18,2},{3,19},{19,3},{4,20},{20... | collective-permute-start | bytes 3981320 | tf_op jit(solution)/shard_map/ppermute | solution.py:96
  372.2 248.0 %all-reduce.13.cloned.1.call-start = ((), (), s32[]{:S(2)}) async-start(), calls=%async_computation.7 | async-start | bytes 8257536 | tf_op jit(solution)/shard_map/psum | solution.py:332
  380.4 65.3 %copy-start.46 = (f32[3,256]{1,0:T(4,128)S(1)}, f32[3,256]{1,0:T(4,128)}, u32[]{:S(2)}) copy-start(f32[3,256]{1,0:T(4,128)} %copy-done.45) | copy-start | bytes 9220
  386.4 62.3 %copy-start.63 = (f32[3,256]{1,0:T(4,128)S(1)}, f32[3,256]{1,0:T(4,128)}, u32[]{:S(2)}) copy-start(f32[3,256]{1,0:T(4,128)} %copy-done.62) | copy-start | bytes 9220
  386.4 62.3 %copy-start.59 = (f32[3,256]{1,0:T(4,128)S(1)}, f32[3,256]{1,0:T(4,128)}, u32[]{:S(2)}) copy-start(f32[3,256]{1,0:T(4,128)} %copy-done.58) | copy-start | bytes 9220
  387.5 72.1 %collective-permute-start.10 = (bf16[576,864]{1,0:T(8,128)(2,1)}, bf16[576,864]{1,0:T(8,128)(2,1)}, u32[]{:S(2)}, u32[]{:S(2)}) collective-permute-start(bf16[576,864]{1,0:T(8,128)(2,1)} %select_convert_fusion.2), channel_id=1, source_target_pairs={{0,16},{16,0},{1,17},{17,1},{2,18},{18,2},{3,19},{19,3},{4,20},{20... | collective-permute-start | bytes 2985992 | tf_op jit(solution)/shard_map/ppermute | solution.py:96
  445.7 7.0 %copy-start.23 = (bf16[768,1152]{1,0:T(8,128)(2,1)S(1)}, bf16[768,1152]{1,0:T(8,128)(2,1)}, u32[]{:S(2)}) copy-start(bf16[768,1152]{1,0:T(8,128)(2,1)} %get-tuple-element.175) | copy-start | bytes 5308420
  445.7 7.0 %copy-start.67 = (f32[1152]{0:T(1024)S(1)}, f32[1152]{0:T(1024)}, u32[]{:S(2)}) copy-start(f32[1152]{0:T(1024)} %param.28) | copy-start | bytes 13828
  458.2 7.7 %collective-permute-start.6 = (f32[24768]{0:T(1024)}, f32[24768]{0:T(1024)}, u32[]{:S(2)}, u32[]{:S(2)}) collective-permute-start(f32[24768]{0:T(1024)} %concatenate.57), channel_id=1, source_target_pairs={{0,4},{4,0},{8,12},{12,8},{1,5},{5,1},{9,13},{13,9},{2,6},{6,2},{1... | collective-permute-start | bytes 297224 | tf_op jit(solution)/shard_map/ppermute | solution.py:96
  463.4 16.4 %copy-start.3 = (bf16[3,256,1152]{2,1,0:T(8,128)(2,1)S(1)}, bf16[3,256,1152]{2,1,0:T(8,128)(2,1)}, u32[]{:S(2)}) copy-start(bf16[3,256,1152]{2,1,0:T(8,128)(2,1)} %param.17) | copy-start | bytes 5308420
  463.4 16.4 %copy-start.9 = (bf16[3,256,1152]{2,1,0:T(8,128)(2,1)S(1)}, bf16[3,256,1152]{2,1,0:T(8,128)(2,1)}, u32[]{:S(2)}) copy-start(bf16[3,256,1152]{2,1,0:T(8,128)(2,1)} %get-tuple-element.176) | copy-start | bytes 5308420
  466.9 11.4 %collective-permute-start.7 = (f32[24768]{0:T(1024)S(1)}, f32[24768]{0:T(1024)S(1)}, u32[]{:S(2)}, u32[]{:S(2)}) collective-permute-start(f32[24768]{0:T(1024)S(1)} %add.234), channel_id=1, source_target_pairs={{0,8},{4,12},{8,0},{12,4},{1,9},{5,13},{9,1},{13,5},{2,10},{6,14},... | collective-permute-start | bytes 297224 | tf_op jit(solution)/shard_map/ppermute | solution.py:96
  478.2 5.6 collective-permute-start.8
  486.5 6.9 %copy-start.49 = (bf16[3,1152]{1,0:T(4,128)(2,1)S(1)}, bf16[3,1152]{1,0:T(4,128)(2,1)}, u32[]{:S(2)}) copy-start(bf16[3,1152]{1,0:T(4,128)(2,1)} %copy-done.48) | copy-start | bytes 20740
  486.5 6.9 %copy-start.51 = (bf16[3,1152]{1,0:T(4,128)(2,1)S(1)}, bf16[3,1152]{1,0:T(4,128)(2,1)}, u32[]{:S(2)}) copy-start(bf16[3,1152]{1,0:T(4,128)(2,1)} %copy-done.50) | copy-start | bytes 20740
  492.0 10.3 %collective-permute-start.9 = (f32[3,576]{1,0:T(4,128)S(1)}, f32[3,576]{1,0:T(4,128)S(1)}, u32[]{:S(2)}, u32[]{:S(2)}) collective-permute-start(f32[3,576]{1,0:T(4,128)S(1)} %slice_select_fusion.3), channel_id=1, source_target_pairs={{0,16},{16,0},{1,17},{17,1},{2,18},{18,2},{3,19},{19,3},{4,20},{20... | collective-permute-start | bytes 20744 | tf_op jit(solution)/shard_map/ppermute | solution.py:96
  493.3 8.9 %copy-start.53 = (bf16[3,1152]{1,0:T(4,128)(2,1)S(1)}, bf16[3,1152]{1,0:T(4,128)(2,1)}, u32[]{:S(2)}) copy-start(bf16[3,1152]{1,0:T(4,128)(2,1)} %param.18) | copy-start | bytes 20740
  (49 other events, 131.8 us)
Sparse Core Ops, SparseCore 0:
  123.6 44.2 all-reduce.6
  192.4 46.0 all-reduce.8
  372.3 73.3 all-reduce.10
  466.0 154.0 all-reduce.12
